TPU v7x, 32 devices: a whole 2x2x4 slice. The times are simulated.
32 devices in a mesh: groups: 2 (over y), pool: 4 (over z), sub: 2 (over x), chip: 2 (over core).
Axes of the slice: x: 2, y: 2, z: 4, core: 2. Of those that a mesh axis runs over, the one named last changes fastest.
Arguments:
- hidden: bfloat16 [1024, 4096], P(('groups', 'pool', 'sub', 'chip')), parts along dimension 0, may hold values from -6 to 6
- query_weight_matrix: bfloat16 [4096, 4096], P(None, 'pool'), may hold values from -0.09375 to 0.09375
- adapter_down_weight: bfloat16 [64, 64, 4096], P('pool', None, ('sub', 'chip')), may hold values from -0.09375 to 0.09375
- adapter_up_weight: bfloat16 [64, 64, 4096], P('pool', None, ('sub', 'chip')), may hold values from -0.75 to 0.75
- adapter_index_rows: int32 [1024], P(('groups', 'pool', 'sub', 'chip')), parts along dimension 0, may hold values from 0 to 63, as said below
Outputs:
- query: bfloat16 [1024, 4096], P(('groups', 'pool', 'sub', 'chip')), parts along dimension 0
There are 2 independent parts, one for each index of `groups`. A program takes and returns all parts, laid end to end along the dimension named above; an argument that names none is the same for every part. Nothing has to cross between parts.
Inputs may be any that keep to these rules, and one draw needn't show every extreme that they name: A row's owner is adapter_index_rows // 16. In each aligned block of 32 rows (the rows of one device) at most 12 rows have one owner, and in every block some owner has exactly 12 rows.
All inputs are finite; a program needn't handle non-finite values.
Results may differ from a plain program's by a relative error of at most 0.0052.
Values may be sent and summed in bfloat16 or wider, within the bound.
A program may use at most 64 MiB of HBM per device.

v0:
```python
import jax
import jax.numpy as jnp
from jax import lax
from jax.sharding import PartitionSpec as P

ADAPTER_SCALE = 0.5


def owner_rank(owner, count):
    table = (owner[:, None] == jnp.arange(count, dtype=jnp.int32)[None, :]).astype(jnp.int32)
    running = jnp.cumsum(table, axis=0) - table
    return jnp.sum(running * table, axis=1)


def reduced_rank_term(incoming_rows, nearby_adapters, adapter_down_weight, adapter_up_weight):
    adapter_stack, rank_extent, portion_width = adapter_down_weight.shape
    flattened_down = adapter_down_weight.reshape(adapter_stack * rank_extent, portion_width)
    project = lax.dot_general(
        incoming_rows, flattened_down, (((1,), (1,)), ((), ())), preferred_element_type=jnp.float32
    )
    select = nearby_adapters[:, None] == jnp.arange(adapter_stack, dtype=jnp.int32)[None, :]
    partial_low = jnp.sum(
        project.reshape(-1, adapter_stack, rank_extent) * select[:, :, None].astype(jnp.float32),
        axis=1,
    )
    projected_down = lax.psum(partial_low, ("sub", "chip")).astype(jnp.bfloat16)
    spread = (select[:, :, None].astype(jnp.bfloat16) * projected_down[:, None, :]).reshape(
        -1, adapter_stack * rank_extent
    )
    flattened_up = adapter_up_weight.reshape(adapter_stack * rank_extent, portion_width)
    update_term = jnp.dot(spread, flattened_up, preferred_element_type=jnp.float32)
    return (ADAPTER_SCALE * update_term).astype(jnp.bfloat16)


def local(hidden, query_weight_matrix, adapter_down_weight, adapter_up_weight, adapter_index_rows):
    pools = lax.axis_size("pool")
    shards = lax.axis_size(("sub", "chip"))
    shard_index = lax.axis_index(("sub", "chip"))
    row_count, width = hidden.shape
    adapter_stack = adapter_down_weight.shape[0]
    portion_width = adapter_down_weight.shape[2]
    capacity = 2 + row_count // (pools - 1)
    nothing = jnp.zeros((), jnp.bfloat16)
    query_cols = jnp.dot(
        lax.all_gather(hidden, "pool", axis=0, tiled=True),
        query_weight_matrix,
        preferred_element_type=jnp.float32,
    ).astype(jnp.bfloat16)
    block_rows, block_adapters = (
        lax.all_gather(hidden, ("sub", "chip"), axis=0, tiled=True),
        lax.all_gather(adapter_index_rows, ("sub", "chip"), axis=0, tiled=True),
    )
    block_size = shards * row_count
    per_owner = shards * capacity
    combined_output = pools * per_owner
    owner = block_adapters // adapter_stack
    slot = owner * per_owner + owner_rank(owner, pools)
    slot_row = (
        jnp.full((combined_output,), -1, jnp.int32)
        .at[slot]
        .set(jnp.arange(block_size, dtype=jnp.int32))
    )
    filled = slot_row >= 0
    safe_row = jnp.maximum(slot_row, 0)
    my_slice = lax.dynamic_slice_in_dim(block_rows, shard_index * portion_width, portion_width, 1)
    send_rows = jnp.where(filled[:, None], jnp.take(my_slice, safe_row, axis=0), nothing)
    send_adapters = jnp.where(filled, jnp.take(block_adapters % adapter_stack, safe_row), 0)
    received_rows, received_adapters = (
        lax.all_to_all(
            send_rows.reshape(pools, per_owner, portion_width),
            "pool",
            split_axis=0,
            concat_axis=0,
            tiled=True,
        ),
        lax.all_to_all(
            send_adapters.reshape(pools, per_owner), "pool", split_axis=0, concat_axis=0, tiled=True
        ),
    )
    update_term = reduced_rank_term(
        received_rows.reshape(combined_output, portion_width),
        received_adapters.reshape(combined_output),
        adapter_down_weight,
        adapter_up_weight,
    )
    returned = lax.all_to_all(
        update_term.reshape(pools, per_owner, portion_width),
        "pool",
        split_axis=0,
        concat_axis=0,
        tiled=True,
    )
    delta_block = jnp.take(returned.reshape(combined_output, portion_width), slot, axis=0)
    delta_rows = lax.all_to_all(
        delta_block, ("sub", "chip"), split_axis=0, concat_axis=1, tiled=True
    )
    query = lax.all_to_all(query_cols, "pool", split_axis=0, concat_axis=1, tiled=True)
    return (query.astype(jnp.float32) + delta_rows.astype(jnp.float32)).astype(jnp.bfloat16)


def solution(mesh):
    in_specs = (
        P(("groups", "pool", "sub", "chip"), None),
        P(None, "pool"),
        P("pool", None, ("sub", "chip")),
        P("pool", None, ("sub", "chip")),
        P(("groups", "pool", "sub", "chip")),
    )
    out_specs = P(("groups", "pool", "sub", "chip"), None)
    return jax.shard_map(local, mesh=mesh, in_specs=in_specs, out_specs=out_specs, check_vma=False)
```

profile of v0, /device:TPU:0, one launch (start us, length us, event | category | flops | bytes accessed | tf_op | source)
XLA Modules:
  0.0 115.8 jit_solution(494919803565934389)
XLA Ops:
  6.5 0.0 copy-start
  6.5 0.0 all-gather.5.cloned.1.call-start
  6.5 0.7 all-gather.5.cloned.1.call-update
  7.3 1.2 %dynamic-slice = u32[1]{0:T(128)} dynamic-slice(u32[32]{0:T(128)} %constant.102, u32[]{:T(128)S(6)} %add.48), dynamic_slice_sizes={1} | dynamic-slice | bytes 12
  9.2 0.9 dynamic-update-slice
  10.0 6.3 %all-reduce = s32[128]{0:T(128)S(1)} all-reduce(s32[128]{0:T(128)S(1)} %dynamic-update-slice), channel_id=1, replica_groups=mesh['groups'=2,'pool'=4,'sub'=2,'chip'=2] {'sub','chip'}, use_global_device_ids=true, to_apply=%add | all-reduce | flops 128 | bytes 1024
  16.4 0.1 fusion.7
  16.5 0.2 reduce_window_sum.11
  16.7 0.2 select_reduce_fusion
  16.9 1.0 scatter_custom_fusion
  17.9 1.6 %gather_fusion = s32[192]{0:T(256)S(1)} fusion(s32[128]{0:T(128)S(1)} %get-tuple-element.12, s32[1024]{0:T(1024)S(1)} %pad_clamp_fusion.1), kind=kCustom, calls=%fused_computation | custom fusion | bytes 2304 | tf_op jit(solution)/shard_map/jit(_take)/gather | solution.py:67
  19.4 0.7 all_to_all.32
  20.1 4.9 %all-to-all-start.1 = ((s32[4,1,48]{2,1,0:T(1,128)}), s32[4,1,48]{2,1,0:T(1,128)S(1)}, u32[]{:S(2)}, u32[]{:S(2)}) async-start(s32[4,1,48]{2,1,0:T(1,128)} %all_to_all.32), calls=%async_computation.1 | async-start | bytes 4096 | tf_op jit(solution)/shard_map/all_to_all | solution.py:76
  25.0 0.0 all-gather.3.cloned.1.call-start
  25.0 0.7 all-gather.3.cloned.1.call-update
  25.7 0.1 broadcast_in_dim.67
  25.8 0.1 broadcast_in_dim.69
  25.9 2.5 %all-gather.5.cloned.1.call-done = bf16[128,4096]{1,0:T(8,128)(2,1)} async-done(((bf16[32,4096]{1,0:T(8,128)(2,1)}), bf16[128,4096]{1,0:T(8,128)(2,1)}) %all-gather.5.cloned.1.call-update) | async-done | bytes 1048592 | tf_op jit(solution)/shard_map/all_gather | solution.py:50
  28.4 1.0 constant_dynamic-slice_fusion
  29.3 1.0 gather_fusion.1
  30.4 0.9 select_select_fusion
  31.2 0.0 all-to-all-done.1
  31.2 4.6 %all-to-all-start.2 = ((bf16[4,48,1024]{2,1,0:T(8,128)(2,1)}), bf16[4,48,1024]{2,1,0:T(8,128)(2,1)S(1)}, u32[]{:S(2)}, u32[]{:S(2)}) async-start(bf16[4,48,1024]{2,1,0:T(8,128)(2,1)} %select_select_fusion), calls=%async_computation.2 | async-start | bytes 786432 | tf_op jit(solution)/shard_map/all_to_all | solution.py:69
  35.8 0.5 broadcast.96
  36.3 0.7 reduce.3
  37.0 0.1 eq.40
  37.1 20.6 %all-to-all-done.2 = bf16[4,48,1024]{2,1,0:T(8,128)(2,1)S(1)} async-done(((bf16[4,48,1024]{2,1,0:T(8,128)(2,1)}), bf16[4,48,1024]{2,1,0:T(8,128)(2,1)S(1)}, u32[]{:S(2)}, u32[]{:S(2)}) %all-to-all-start.2) | async-done | bytes 393248 | tf_op jit(solution)/shard_map/all_to_all | solution.py:69
  57.7 2.3 %fusion.2 = f32[192,64]{0,1:T(8,128)S(1)} fusion(bf16[192,1024,1]{1,0,2:T(8,128)(2,1)S(1)} %bitcast.27, bf16[16,64,1024]{2,1,0:T(8,128)(2,1)} %param.7, f32[192,16]{0,1:T(8,128)S(1)} %get-tuple-element.11), kind=kOutput, calls=%fused_computation.8 | convolution fusion | flops 403034112 | bytes 2551808 | tf_op jit(solution)/shard_map/dot_general | solution.py:18
  60.1 11.1 %psum.7 = bf16[192,64]{0,1:T(8,128)(2,1)S(1)} all-reduce(f32[192,64]{0,1:T(8,128)S(1)} %fusion.2), channel_id=1, replica_groups=mesh['groups'=2,'pool'=4,'sub'=2,'chip'=2] {'sub','chip'}, use_global_device_ids=true, to_apply=%region_4.5 | all-reduce | flops 12288 | bytes 73728 | tf_op jit(solution)/shard_map/psum | solution.py:26
  71.1 0.0 copy-done
  71.2 1.4 %fusion.1 = bf16[192,1024]{1,0:T(8,128)(2,1)} fusion(bf16[16,64,1024]{2,1,0:T(8,128)(2,1)S(1)} %copy-done, bf16[192,64]{0,1:T(8,128)(2,1)S(1)} %psum.7, bf16[192,16]{0,1:T(8,128)(2,1)S(1)} %get-tuple-element.10), kind=kOutput, calls=%fused_computation.7 | convolution fusion | flops 403243008 | bytes 2521088 | tf_op jit(solution)/shard_map/dot_general | solution.py:31
  72.5 3.5 %all-to-all-start.3 = ((bf16[4,48,1024]{2,1,0:T(8,128)(2,1)}), bf16[4,48,1024]{2,1,0:T(8,128)(2,1)S(1)}, u32[]{:S(2)}, u32[]{:S(2)}) async-start(bf16[4,48,1024]{2,1,0:T(8,128)(2,1)} %bitcast.6), calls=%async_computation.3 | async-start | bytes 786432 | tf_op jit(solution)/shard_map/all_to_all | solution.py:86
  76.0 0.0 all-gather.3.cloned.1.call-done
  76.0 5.7 %convolution_convert_fusion = bf16[128,1024]{1,0:T(8,128)(2,1)} fusion(bf16[128,4096]{1,0:T(8,128)(2,1)} %all-gather.3.cloned.1.call-done, bf16[4096,1024]{1,0:T(8,128)(2,1)} %param.6), kind=kOutput, calls=%fused_computation.9 | convolution fusion | flops 1073872896 | bytes 9699328 | tf_op jit(solution)/shard_map/dot_general | solution.py:44
  81.7 5.7 %all-to-all-done.3 = bf16[4,48,1024]{2,1,0:T(8,128)(2,1)S(1)} async-done(((bf16[4,48,1024]{2,1,0:T(8,128)(2,1)}), bf16[4,48,1024]{2,1,0:T(8,128)(2,1)S(1)}, u32[]{:S(2)}, u32[]{:S(2)}) %all-to-all-start.3) | async-done | bytes 393248 | tf_op jit(solution)/shard_map/all_to_all | solution.py:86
  87.4 3.4 %all-to-all-start = ((bf16[4,32,1024]{2,1,0:T(8,128)(2,1)}), bf16[4,32,1024]{2,1,0:T(8,128)(2,1)S(1)}, u32[]{:S(2)}, u32[]{:S(2)}) async-start(bf16[4,32,1024]{2,1,0:T(8,128)(2,1)} %bitcast), calls=%async_computation | async-start | bytes 524288 | tf_op jit(solution)/shard_map/all_to_all | solution.py:97
  90.8 0.1 broadcast_in_dim.61
  90.9 0.9 gather_fusion.2
  91.7 0.1 broadcast_select_fusion
  91.8 5.7 %all-to-all-done = bf16[4,32,1024]{2,1,0:T(8,128)(2,1)S(1)} async-done(((bf16[4,32,1024]{2,1,0:T(8,128)(2,1)}), bf16[4,32,1024]{2,1,0:T(8,128)(2,1)S(1)}, u32[]{:S(2)}, u32[]{:S(2)}) %all-to-all-start) | async-done | bytes 262176 | tf_op jit(solution)/shard_map/all_to_all | solution.py:97
  97.5 10.6 %all_to_all.42 = bf16[4,32,1024]{2,1,0:T(8,128)(2,1)S(1)} all-to-all(bf16[4,32,1024]{2,1,0:T(8,128)(2,1)S(1)} %broadcast_select_fusion), channel_id=1, replica_groups=mesh['groups'=2,'pool'=4,'sub'=2,'chip'=2] {'sub','chip'}, dimensions={0} | all-to-all | bytes 524288 | tf_op jit(solution)/shard_map/all_to_all | solution.py:94
  108.2 0.1 fusion.4
  108.2 0.7 copy.11
  (9 shorter events, 0.1 us)
Async XLA Ops:
  6.5 64.6 %copy-start = (bf16[16,64,1024]{2,1,0:T(8,128)(2,1)S(1)}, bf16[16,64,1024]{2,1,0:T(8,128)(2,1)}, u32[]{:S(2)}) copy-start(bf16[16,64,1024]{2,1,0:T(8,128)(2,1)} %param.8) | copy-start | bytes 6291460
  6.5 21.8 %all-gather.5.cloned.1.call-start = ((), (), s32[]{:S(2)}) async-start(), calls=%async_computation.6 | async-start | bytes 1310720 | tf_op jit(solution)/shard_map/all_gather | solution.py:50
  20.1 11.1 %all-to-all-start.1 = ((s32[4,1,48]{2,1,0:T(1,128)}), s32[4,1,48]{2,1,0:T(1,128)S(1)}, u32[]{:S(2)}, u32[]{:S(2)}) async-start(s32[4,1,48]{2,1,0:T(1,128)} %all_to_all.32), calls=%async_computation.1 | async-start | bytes 4096 | tf_op jit(solution)/shard_map/all_to_all | solution.py:76
  25.0 51.0 %all-gather.3.cloned.1.call-start = ((), (), s32[]{:S(2)}) async-start(), calls=%async_computation.5 | async-start | bytes 1310720 | tf_op jit(solution)/shard_map/all_gather | solution.py:45
  31.2 26.5 %all-to-all-start.2 = ((bf16[4,48,1024]{2,1,0:T(8,128)(2,1)}), bf16[4,48,1024]{2,1,0:T(8,128)(2,1)S(1)}, u32[]{:S(2)}, u32[]{:S(2)}) async-start(bf16[4,48,1024]{2,1,0:T(8,128)(2,1)} %select_select_fusion), calls=%async_computation.2 | async-start | bytes 786432 | tf_op jit(solution)/shard_map/all_to_all | solution.py:69
  72.5 14.8 %all-to-all-start.3 = ((bf16[4,48,1024]{2,1,0:T(8,128)(2,1)}), bf16[4,48,1024]{2,1,0:T(8,128)(2,1)S(1)}, u32[]{:S(2)}, u32[]{:S(2)}) async-start(bf16[4,48,1024]{2,1,0:T(8,128)(2,1)} %bitcast.6), calls=%async_computation.3 | async-start | bytes 786432 | tf_op jit(solution)/shard_map/all_to_all | solution.py:86
  87.4 10.2 %all-to-all-start = ((bf16[4,32,1024]{2,1,0:T(8,128)(2,1)}), bf16[4,32,1024]{2,1,0:T(8,128)(2,1)S(1)}, u32[]{:S(2)}, u32[]{:S(2)}) async-start(bf16[4,32,1024]{2,1,0:T(8,128)(2,1)} %bitcast), calls=%async_computation | async-start | bytes 524288 | tf_op jit(solution)/shard_map/all_to_all | solution.py:97
Sparse Core Ops, SparseCore 0:
  8.9 19.4 all-gather.4
  29.9 35.1 all-gather.2
where the time goes:
time: 116 us
  waiting for transfers between devices  35.9 us (31%)
  blocking collectives  28.1 us (24%)
  starting transfers between devices  16.3 us (14%)
  between operations  14.2 us (12%)
  local copies, waits for them, and re-layouts  9.72 us (8%)
  matrix products  9.37 us (8%)
  other arithmetic  2.18 us (2%)
    all_to_all x1, waiting for transfers between devices, local(): lax.all_to_all(send_rows.reshape(pools, per_owner, portion_width), 'pool'...  20.6 us
    psum x1, blocking collectives, reduced_rank_term(): projected_down = lax.psum(partial_low, ('sub', 'chip')).astype(jnp.bfloat16)  11.1 us
    all_to_all x1, blocking collectives, local(): lax.all_to_all(delta_block, ('sub', 'chip'), split_axis=0, concat_axis=1,...  10.6 us
    unnamed x1, blocking collectives  6.35 us
    all_to_all x1, waiting for transfers between devices, local(): lax.all_to_all(query_cols, 'pool', split_axis=0, concat_axis=1, tiled=True)  5.69 us
    dot_general x1, matrix products, local(): jnp.dot(lax.all_gather(hidden, 'pool', axis=0, tiled=True), query_weight_...  5.68 us
    all_to_all x1, waiting for transfers between devices, local(): lax.all_to_all(update_term.reshape(pools, per_owner, portion_width), 'poo...  5.67 us
    all_to_all x1, starting transfers between devices, local(): lax.all_to_all(send_adapters.reshape(pools, per_owner), 'pool', split_axi...  4.87 us
  transfers between devices with their start and end apart: 6, of which 4 were waited for; matrix products, arithmetic and copies ran while one was open for 17% of the time, Pallas kernels for 0%

commit v1 on v0

v1 whole, which is shorter than its diff:
```python
import functools

import jax
import jax.numpy as jnp
from jax import lax
from jax.experimental import pallas as pl
from jax.experimental.pallas import tpu as pltpu
from jax.sharding import PartitionSpec as P

ADAPTER_SCALE = 0.5
SLOTS = 16
MESH = pl.DeviceIdType.MESH
F32 = jnp.float32
BF16 = jnp.bfloat16


def tile_of(extent):
    return 256 if extent % 256 == 0 else extent


def kernel(
    pools, chips, shards, stack,
    h_ref, idx_ref, col_ref, w_hbm, dn_hbm, up_hbm, out_ref,
    x, w, dn, up, ids, picked, rows, low_out, low, delta, home_delta, base, home_base, acc,
    wsem, isend, irecv, hright, hleft, hrecv, rsend, rrecv, lsend, lrecv, bsend, brecv, dsend, drecv,
):
    p = lax.axis_index("pool")
    me = lax.axis_index("sub") * chips + lax.axis_index("chip")
    rows_dev, width = h_ref.shape
    cols = w.shape[1]
    part = width // shards
    half = width // 2
    ranks = dn.shape[0] // stack
    many = shards * SLOTS

    def rcopy(src, dst, ssem, rsem, z, sh):
        return pltpu.make_async_remote_copy(
            src_ref=src, dst_ref=dst, send_sem=ssem, recv_sem=rsem,
            device_id={"pool": z, "sub": sh // chips, "chip": sh % chips},
            device_id_type=MESH,
        )

    def others(f):
        def step(z, carry):
            for sh in range(shards):
                @pl.when(jnp.logical_or(z != p, sh != me))
                def _():
                    f(z, sh)
            return carry
        lax.fori_loop(0, pools, step, 0)

    loads = [
        pltpu.make_async_copy(w_hbm.at[pl.ds(0, half)], w.at[pl.ds(0, half)], wsem.at[0]),
        pltpu.make_async_copy(w_hbm.at[pl.ds(half, half)], w.at[pl.ds(half, half)], wsem.at[1]),
        pltpu.make_async_copy(dn_hbm, dn, wsem.at[2]),
        pltpu.make_async_copy(up_hbm, up, wsem.at[3]),
    ]
    for load in (loads[2], loads[0], loads[3], loads[1]):
        load.start()

    barrier = pltpu.get_barrier_semaphore()

    def greet(z, sh):
        pl.semaphore_signal(
            barrier, inc=1,
            device_id={"pool": z, "sub": sh // chips, "chip": sh % chips}, device_id_type=MESH,
        )

    others(greet)
    pl.semaphore_wait(barrier, pools * shards - 1)

    mine = p * shards + me

    def id_copy(z, sh):
        return rcopy(idx_ref, ids.at[mine], isend.at[z * shards + sh], irecv.at[mine], z, sh)

    others(lambda z, sh: id_copy(z, sh).start())

    def piece(q):
        return pl.ds(q * part, part)

    def to_right(src, b, q):
        return rcopy(src, x.at[b, :, piece(q)], hright.at[b, q], hrecv.at[b, q], p + 1, me)

    def to_left(src, b, q):
        return rcopy(src, x.at[b, :, piece(q)], hleft.at[b, q], hrecv.at[b, q], p - 1, me)

    for q in range(shards):
        @pl.when(p + 1 < pools)
        def _():
            to_right(h_ref.at[:, piece(q)], p, q).start()

        @pl.when(p >= 1)
        def _():
            to_left(h_ref.at[:, piece(q)], p, q).start()

    x[p] = h_ref[...]
    ids[mine] = idx_ref[...]

    def id_wait(z, sh):
        g = z * shards + sh
        rcopy(idx_ref, ids.at[g], isend.at[g], irecv.at[g], z, sh).wait_recv()

    others(id_wait)

    def selection(g):
        number = jnp.broadcast_to(ids[g][:, :rows_dev], (SLOTS, rows_dev)) - p * stack
        owned = jnp.logical_and(number >= 0, number < stack)
        before = (
            lax.broadcasted_iota(jnp.int32, (rows_dev, rows_dev), 0)
            < lax.broadcasted_iota(jnp.int32, (rows_dev, rows_dev), 1)
        )
        rank = jnp.dot(
            jnp.where(owned, 1.0, 0.0).astype(BF16), jnp.where(before, 1.0, 0.0).astype(BF16),
            preferred_element_type=F32,
        )
        slot = lax.broadcasted_iota(jnp.int32, (SLOTS, rows_dev), 0).astype(F32)
        hit = jnp.logical_and(owned, rank == slot)
        return jnp.where(hit, 1.0, 0.0), number.astype(F32)

    def pick(b, chosen, q):
        got = jnp.dot(chosen, x[b, :, piece(q)], preferred_element_type=F32).astype(BF16)

        @pl.when(q != me)
        def _():
            picked[b, q] = got
            rcopy(picked.at[b, q], rows.at[b, me], rsend.at[b, q], rrecv.at[b, me], p, q).start()

        @pl.when(q == me)
        def _():
            rows[b, me] = got

    def receive(b, from_left):
        chosen = selection(b * shards + me)[0].astype(BF16)
        for q in range(shards):
            dst = x.at[b, :, piece(q)]
            rcopy(dst, dst, hright.at[b, q], hrecv.at[b, q], p, (me + 1) % shards).wait_recv()
            if from_left:
                @pl.when(p + 1 < pools)
                def _():
                    to_right(x.at[b, :, piece(q)], b, q).start()
            else:
                @pl.when(p >= 1)
                def _():
                    to_left(x.at[b, :, piece(q)], b, q).start()
            pick(b, chosen, q)

    def peers():
        return [(me + d) % shards for d in range(1, shards)]

    def project(b, k, last):
        tile = tile_of(cols)

        def step(j, carry):
            at = pl.ds(pl.multiple_of(j * tile, tile), tile)
            term = jnp.dot(
                x[b, :, pl.ds(k * half, half)], w[pl.ds(k * half, half), at],
                preferred_element_type=F32,
            )
            if last:
                base[b, :, at] = (acc[:, at] + term).astype(BF16)
            else:
                acc[:, at] = term
            return carry

        lax.fori_loop(0, cols // tile, step, 0)

    mine_cols = pl.ds(pl.multiple_of(p * cols, 128), cols)

    def base_copy(b):
        return rcopy(base.at[b], home_base.at[:, mine_cols], bsend.at[b], brecv.at[p], b, me)

    def delta_copy(b, sh):
        return rcopy(
            delta.at[b, sh], home_delta.at[me, pl.ds(pl.multiple_of(p * SLOTS, SLOTS), SLOTS)],
            dsend.at[b, sh], drecv.at[p, me], b, sh,
        )

    def process(b, own):
        if own:
            loads[0].wait()
        project(b, 0, False)

        parts = []
        for sh in range(shards):
            hit, number = selection(b * shards + sh)
            parts.append(jnp.sum(hit * number, axis=1, keepdims=True))
        adapter = jnp.concatenate(parts, axis=0).astype(jnp.int32)

        for sh in peers():
            rcopy(rows.at[b, sh], rows.at[b, sh], rsend.at[b, sh], rrecv.at[b, sh], p, sh).wait_recv()
        if own:
            loads[2].wait()
        here = rows[b].reshape(many, part)
        lane = lax.broadcasted_iota(jnp.int32, (many, 256), 1) // ranks
        each = 256 // ranks
        total = jnp.zeros((many, 128), F32)
        for j in range(stack * ranks // 256):
            term = lax.dot_general(
                here, dn[pl.ds(j * 256, 256), :], (((1,), (1,)), ((), ())),
                preferred_element_type=F32,
            )
            term = jnp.where(lane + j * each == adapter, term, 0.0)
            total = total + term[:, :128] + term[:, 128:]
        total = total + pltpu.roll(total, 64, 1)
        lower = lax.broadcasted_iota(jnp.int32, (many // 2, 128), 1) < 64
        packed = jnp.where(lower, total[: many // 2], total[many // 2 :])
        low_out[b] = packed
        low[b, me] = packed
        for sh in peers():
            rcopy(low_out.at[b], low.at[b, me], lsend.at[b, sh], lrecv.at[b, me], p, sh).start()

        if own:
            loads[1].wait()
        project(b, 1, True)
        if own:
            home_base[:, mine_cols] = base[b]
        else:
            base_copy(b).start()

        for sh in peers():
            rcopy(low_out.at[b], low.at[b, sh], lsend.at[b, sh], lrecv.at[b, sh], p, sh).wait_recv()
        both = low[b, 0]
        for sh in range(1, shards):
            both = both + low[b, sh]
        both = both.astype(BF16).astype(F32)
        turned = pltpu.roll(both, 64, 1)
        full = jnp.concatenate(
            [jnp.where(lower, both, turned), jnp.where(lower, turned, both)], axis=0
        )
        full = jnp.concatenate([full, full], axis=1)
        spread = jnp.concatenate(
            [
                jnp.where(lane + j * each == adapter, full, 0.0).astype(BF16)
                for j in range(stack * ranks // 256)
            ],
            axis=1,
        )
        if own:
            loads[3].wait()
        for j in range(part // 256):
            at = pl.ds(j * 256, 256)
            term = jnp.dot(spread, up[:, at], preferred_element_type=F32)
            delta[b, :, :, at] = (ADAPTER_SCALE * term).astype(BF16).reshape(shards, SLOTS, 256)
        for sh in range(shards):
            if own:
                @pl.when(sh != me)
                def _():
                    delta_copy(b, sh).start()

                @pl.when(sh == me)
                def _():
                    home_delta[me, pl.ds(pl.multiple_of(p * SLOTS, SLOTS), SLOTS)] = delta[b, sh]
            else:
                delta_copy(b, sh).start()

    chosen_here = selection(mine)[0].astype(BF16)
    for q in range(shards):
        pick(p, chosen_here, q)
    process(p, True)

    def receive_step(t):
        @pl.when(p - 1 - t >= 0)
        def _():
            receive(p - 1 - t, True)

        @pl.when(p + 1 + t < pools)
        def _():
            receive(p + 1 + t, False)

    receive_step(0)

    def step(t, carry):
        left = p - 1 - t >= 0
        right = p + 1 + t < pools

        def turn(i, c):
            b = jnp.where(i == 0, p - 1 - t, p + 1 + t)

            @pl.when(jnp.logical_and(b >= 0, b < pools))
            def _():
                process(b, False)

            @pl.when(i == jnp.where(jnp.logical_and(left, right), 0, 1))
            def _():
                receive_step(t + 1)
            return c

        return lax.fori_loop(0, 2, turn, carry)

    lax.fori_loop(0, pools - 1, step, 0)

    column = col_ref[...]
    slots = pools * SLOTS
    lanes = lax.broadcasted_iota(jnp.int32, (rows_dev, slots), 1)
    owner = jnp.where(column // stack == lanes // SLOTS, 1.0, 0.0)
    after = (
        lax.broadcasted_iota(jnp.int32, (rows_dev, rows_dev), 0)
        > lax.broadcasted_iota(jnp.int32, (rows_dev, rows_dev), 1)
    )
    rank = jnp.dot(
        jnp.where(after, 1.0, 0.0).astype(BF16), owner.astype(BF16), preferred_element_type=F32
    )
    place = jnp.where(rank == (lanes % SLOTS).astype(F32), owner, 0.0).astype(BF16)

    def base_wait(z, carry):
        @pl.when(z != p)
        def _():
            dst = home_base.at[:, pl.ds(pl.multiple_of(z * cols, 128), cols)]
            rcopy(base.at[z], dst, bsend.at[z], brecv.at[z], z, me).wait_recv()
        return carry

    lax.fori_loop(0, pools, base_wait, 0)

    def delta_wait(z, sh):
        dst = home_delta.at[sh, pl.ds(pl.multiple_of(z * SLOTS, SLOTS), SLOTS)]
        rcopy(delta.at[z, sh], dst, dsend.at[z, sh], drecv.at[z, sh], z, sh).wait_recv()

    others(delta_wait)
    for sh in range(shards):
        term = jnp.dot(place, home_delta[sh], preferred_element_type=F32)
        out_ref[:, piece(sh)] = (home_base[:, piece(sh)].astype(F32) + term).astype(BF16)

    others(lambda z, sh: id_copy(z, sh).wait_send())
    others(lambda z, sh: delta_copy(z, sh).wait_send())

    def drain(b, carry):
        for q in range(shards):
            @pl.when(jnp.logical_and(b <= p, p + 1 < pools))
            def _():
                to_right(x.at[b, :, piece(q)], b, q).wait_send()

            @pl.when(jnp.logical_and(b >= p, p >= 1))
            def _():
                to_left(x.at[b, :, piece(q)], b, q).wait_send()

            @pl.when(q != me)
            def _():
                rcopy(picked.at[b, q], rows.at[b, me], rsend.at[b, q], rrecv.at[b, me], p, q).wait_send()
                rcopy(low_out.at[b], low.at[b, me], lsend.at[b, q], lrecv.at[b, me], p, q).wait_send()

        @pl.when(b != p)
        def _():
            base_copy(b).wait_send()
        return carry

    lax.fori_loop(0, pools, drain, 0)


def local(hidden, query_weight_matrix, adapter_down_weight, adapter_up_weight, adapter_index_rows):
    pools = lax.axis_size("pool")
    chips = lax.axis_size("chip")
    shards = lax.axis_size("sub") * chips
    row_count, width = hidden.shape
    cols = query_weight_matrix.shape[1]
    stack, ranks, part = adapter_down_weight.shape
    dma = pltpu.SemaphoreType.DMA
    vmem = pl.BlockSpec(memory_space=pltpu.VMEM)
    hbm = pl.BlockSpec(memory_space=pl.ANY)
    index_line = jnp.pad(adapter_index_rows[None, :], ((0, 0), (0, 128 - row_count)))
    return pl.pallas_call(
        functools.partial(kernel, pools, chips, shards, stack),
        out_shape=jax.ShapeDtypeStruct((row_count, width), BF16),
        in_specs=[vmem, vmem, vmem, hbm, hbm, hbm],
        out_specs=vmem,
        scratch_shapes=[
            pltpu.VMEM((pools, row_count, width), BF16),
            pltpu.VMEM((width, cols), BF16),
            pltpu.VMEM((stack * ranks, part), BF16),
            pltpu.VMEM((stack * ranks, part), BF16),
            pltpu.VMEM((pools * shards, 1, 128), jnp.int32),
            pltpu.VMEM((pools, shards, SLOTS, part), BF16),
            pltpu.VMEM((pools, shards, SLOTS, part), BF16),
            pltpu.VMEM((pools, shards * SLOTS // 2, 128), F32),
            pltpu.VMEM((pools, shards, shards * SLOTS // 2, 128), F32),
            pltpu.VMEM((pools, shards, SLOTS, part), BF16),
            pltpu.VMEM((shards, pools * SLOTS, part), BF16),
            pltpu.VMEM((pools, row_count, cols), BF16),
            pltpu.VMEM((row_count, width), BF16),
            pltpu.VMEM((row_count, cols), F32),
            dma((4,)),
            dma((pools * shards,)),
            dma((pools * shards,)),
            dma((pools, shards)),
            dma((pools, shards)),
            dma((pools, shards)),
            dma((pools, shards)),
            dma((pools, shards)),
            dma((pools, shards)),
            dma((pools, shards)),
            dma((pools,)),
            dma((pools,)),
            dma((pools, shards)),
            dma((pools, shards)),
        ],
        compiler_params=pltpu.CompilerParams(
            collective_id=0, has_side_effects=True, vmem_limit_bytes=56 * 1024 * 1024
        ),
    )(
        hidden,
        index_line,
        adapter_index_rows[:, None],
        query_weight_matrix,
        adapter_down_weight.reshape(stack * ranks, part),
        adapter_up_weight.reshape(stack * ranks, part),
    )


def solution(mesh):
    in_specs = (
        P(("groups", "pool", "sub", "chip"), None),
        P(None, "pool"),
        P("pool", None, ("sub", "chip")),
        P("pool", None, ("sub", "chip")),
        P(("groups", "pool", "sub", "chip")),
    )
    out_specs = P(("groups", "pool", "sub", "chip"), None)
    return jax.shard_map(local, mesh=mesh, in_specs=in_specs, out_specs=out_specs, check_vma=False)
```

time: 116 us -> 55.5 us (0.48)
  Pallas kernels: 0 us -> 50.6 us
  waiting for transfers between devices: 35.9 us -> 0 us
  blocking collectives: 28.1 us -> 0 us
  starting transfers between devices: 16.3 us -> 0 us
  between operations: 14.2 us -> 0.01 us
  matrix products: 9.37 us -> 0 us
  local copies, waits for them, and re-layouts: 9.72 us -> 4.24 us
  other arithmetic: 2.18 us -> 0 us
    pallas_call x0 -> x1, Pallas kernels: none -> 50.6 us  [local(): pl.pallas_call(functools.partial(kernel, pools, chips, shards, stack), ou...]
    all_to_all x4 -> x0, waiting for transfers between devices: 32 us -> none  [the longest x1 20.6 us: local(): lax.all_to_all(send_rows.reshape(pools, per_owner, portion_width), 'pool'...]
    all_to_all x4 -> x0, starting transfers between devices: 16.3 us -> none  [the longest x1 4.87 us: local(): lax.all_to_all(send_adapters.reshape(pools, per_owner), 'pool', split_axi...]
    psum x1 -> x0, blocking collectives: 11.1 us -> none  [reduced_rank_term(): projected_down = lax.psum(partial_low, ('sub', 'chip')).astype(jnp.bfloat16)]
    all_to_all x1 -> x0, blocking collectives: 10.6 us -> none  [local(): lax.all_to_all(delta_block, ('sub', 'chip'), split_axis=0, concat_axis=1,...]
    dot_general x3 -> x0, matrix products: 9.37 us -> none  [the longest x1 5.68 us: local(): jnp.dot(lax.all_gather(hidden, 'pool', axis=0, tiled=True), query_weight_...]
    unnamed x1 -> x0, blocking collectives: 6.35 us -> none
    gather x3 -> x0, local copies, waits for them, and re-layouts: 3.43 us -> none  [the longest x1 1.55 us: local(): jnp.take(block_adapters % adapter_stack, safe_row)]
  transfers between devices with their start and end apart: 6 -> 0, of which waited for: 4 -> 0; matrix products, arithmetic and copies ran while one was open for 17% -> 0% of each run, Pallas kernels for 0% -> 0%
where the time goes in v1:
time: 55.5 us; the launch traced here: 54.8 us
  Pallas kernels  50.6 us (91%)
  local copies, waits for them, and re-layouts  4.24 us (8%)
    pallas_call x1, Pallas kernels, local(): pl.pallas_call(functools.partial(kernel, pools, chips, shards, stack), ou...  50.6 us
    unnamed x1, local copies, waits for them, and re-layouts  1.67 us
    broadcast_in_dim x1, local copies, waits for them, and re-layouts, local(): adapter_index_rows[:, None]  1.34 us
    pad x1, local copies, waits for them, and re-layouts, local(): jnp.pad(adapter_index_rows[None, :], ((0, 0), (0, 128 - row_count)))  1.23 us

profile of v1, /device:TPU:0, one launch (start us, length us, event | category | flops | bytes accessed | tf_op | source)
XLA Modules:
  0.0 54.8 jit_solution(17065408340363417401)
XLA Ops:
  0.0 1.2 %pad.4.idx_ref = s32[1,128]{1,0:T(1,128)} pad(s32[1,32]{1,0:T(1,128)} %bitcast.6, s32[]{:T(128)} %constant.0.clone.1), padding=0_0x0_96 | pad | bytes 644 | tf_op jit(solution)/shard_map/jit(_pad)/pad | solution.py:360
  1.2 1.3 %copy.6.col_ref = s32[32,1]{1,0:T(8,128)} copy(s32[32,1]{0,1:T(1,128)} %bitcast.7) | data formatting | bytes 256 | tf_op jit(solution)/shard_map/broadcast_in_dim | solution.py:402
  2.6 50.6 %shard_map.55 = bf16[32,4096]{1,0:T(8,128)(2,1)} custom-call(bf16[32,4096]{1,0:T(8,128)(2,1)} %h_ref.1, s32[1,128]{1,0:T(1,128)} %pad.4.idx_ref, s32[32,1]{1,0:T(8,128)} %copy.6.col_ref, bf16[4096,1024]{1,0:T(8,128)(2,1)} %w_hbm.1, bf16[1024,1024]{1,0:T(8,128)(2,1)} %bitcast.4, bf16[1024,1024]{1,0:T(8,128)(2,1)} %bitcast.5), custom_call_target="tpu_custom_call" | custom-call | tf_op jit(solution)/shard_map/pallas_call | solution.py:361
  53.1 1.7 %copy.8 = bf16[32,4096]{1,0:T(8,128)(2,1)} copy(bf16[32,4096]{1,0:T(8,128)(2,1)} %shard_map.55) | data formatting | bytes 524288

commit v2 on v1

v2 whole, which is shorter than its diff:
```python
import functools

import jax
import jax.numpy as jnp
from jax import lax
from jax.experimental import pallas as pl
from jax.experimental.pallas import tpu as pltpu
from jax.sharding import PartitionSpec as P

ADAPTER_SCALE = 0.5
SLOTS = 16
HELD = 12
META = 128
MESH = pl.DeviceIdType.MESH
F32 = jnp.float32
BF16 = jnp.bfloat16


def tile_of(extent):
    return 256 if extent % 256 == 0 else extent


def kernel(
    pools, chips, shards, stack,
    h_hbm, idx_ref, w_hbm, dn_hbm, up_hbm, out_ref,
    x, w, dn, up, picked, rows, low_out, low, delta, home_delta, base, home_base, acc,
    wsem, hright, hleft, hrecv, rsend, rrecv, lsend, lrecv, bsend, brecv, dsend, drecv,
):
    p = lax.axis_index("pool")
    me = lax.axis_index("sub") * chips + lax.axis_index("chip")
    rows_dev, width = h_hbm.shape
    cols = w.shape[1]
    part = width // shards
    half = width // 2
    quarter = part // 4
    ranks = dn.shape[0] // stack
    tiles = stack * ranks // 256
    each = 256 // ranks
    many = shards * SLOTS

    def where_is(z, sh):
        return {"pool": z, "sub": sh // chips, "chip": sh % chips}

    def rcopy(src, dst, ssem, rsem, z, sh):
        return pltpu.make_async_remote_copy(
            src_ref=src, dst_ref=dst, send_sem=ssem, recv_sem=rsem,
            device_id=where_is(z, sh), device_id_type=MESH,
        )

    peers = [(me + d) % shards for d in range(1, shards)]

    barrier = pltpu.get_barrier_semaphore()

    def greet(z, sh):
        pl.semaphore_signal(barrier, inc=1, device_id=where_is(z, sh), device_id_type=MESH)

    @pl.when(p >= 1)
    def _():
        greet(p - 1, me)

    @pl.when(p + 1 < pools)
    def _():
        greet(p + 1, me)

    for sh in peers:
        greet(p, sh)

    loads = [
        pltpu.make_async_copy(w_hbm.at[pl.ds(0, half)], w.at[pl.ds(0, half)], wsem.at[0]),
        pltpu.make_async_copy(w_hbm.at[pl.ds(half, half)], w.at[pl.ds(half, half)], wsem.at[1]),
        pltpu.make_async_copy(dn_hbm, dn, wsem.at[2]),
        pltpu.make_async_copy(up_hbm, up, wsem.at[3]),
        pltpu.make_async_copy(h_hbm, x.at[p, :, pl.ds(META, width)], wsem.at[4]),
    ]
    for i in (4, 0, 2, 1, 3):
        loads[i].start()

    square = (rows_dev, rows_dev)
    down_axis = lax.broadcasted_iota(jnp.int32, square, 0)
    along = lax.broadcasted_iota(jnp.int32, square, 1)
    index = jnp.broadcast_to(idx_ref[...], square).astype(F32)
    column = jnp.sum(jnp.where(down_axis == along, index, 0.0), axis=1, keepdims=True)
    column = column.astype(jnp.int32)
    owner_column = column // stack
    first = lax.broadcasted_iota(jnp.int32, (rows_dev, META), 1) == 0
    meta = jnp.where(first, owner_column, column - owner_column * stack)
    x[p, :, pl.ds(0, META)] = meta.astype(F32).astype(BF16)

    greeters = jnp.minimum(p, 1) + jnp.minimum(pools - 1 - p, 1) + shards - 1
    pl.semaphore_wait(barrier, greeters)
    loads[4].wait()

    def piece(q):
        return pl.ds(META + q * part, part)

    def sent(q):
        return pl.ds(0, META + part) if q == 0 else piece(q)

    def to_right(b, q):
        ref = x.at[b, :, sent(q)]
        return rcopy(ref, ref, hright.at[b, q], hrecv.at[b, q], p + 1, me)

    def to_left(b, q):
        ref = x.at[b, :, sent(q)]
        return rcopy(ref, ref, hleft.at[b, q], hrecv.at[b, q], p - 1, me)

    for q in range(shards):
        @pl.when(p + 1 < pools)
        def _():
            to_right(p, q).start()

        @pl.when(p >= 1)
        def _():
            to_left(p, q).start()

    before = jnp.where(down_axis < along, 1.0, 0.0).astype(BF16)

    def selection(b):
        pick_owner = lax.broadcasted_iota(jnp.int32, (SLOTS, META), 1) == 0
        owner = lax.dot_general(
            jnp.where(pick_owner, 1.0, 0.0).astype(BF16), x[b, :, pl.ds(0, META)],
            (((1,), (1,)), ((), ())), preferred_element_type=F32,
        )
        owned = jnp.where(owner == p.astype(F32), 1.0, 0.0)
        rank = jnp.dot(owned.astype(BF16), before, preferred_element_type=F32)
        slot = lax.broadcasted_iota(jnp.int32, (SLOTS, rows_dev), 0).astype(F32)
        return jnp.where(rank == slot, owned, 0.0).astype(BF16)

    def pick(b, chosen, tag, q):
        got = jnp.dot(chosen, x[b, :, piece(q)], preferred_element_type=F32).astype(BF16)

        @pl.when(q != me)
        def _():
            picked[b, q, :, pl.ds(0, META)] = tag
            picked[b, q, :, pl.ds(META, part)] = got
            rcopy(picked.at[b, q], rows.at[b, me], rsend.at[b, q], rrecv.at[b, me], p, q).start()

        @pl.when(q == me)
        def _():
            rows[b, me, :, pl.ds(0, META)] = tag
            rows[b, me, :, pl.ds(META, part)] = got

    def select_tag(b):
        chosen = selection(b)
        tag = jnp.dot(chosen, x[b, :, pl.ds(0, META)], preferred_element_type=F32).astype(BF16)
        return chosen, tag

    def arrive(b, q, from_left):
        rcopy(
            x.at[b, :, sent(q)], x.at[b, :, sent(q)], hright.at[b, q], hrecv.at[b, q], p, peers[0]
        ).wait_recv()
        if from_left:
            @pl.when(p + 1 < pools)
            def _():
                to_right(b, q).start()
        else:
            @pl.when(p >= 1)
            def _():
                to_left(b, q).start()

    def receive(b, from_left):
        arrive(b, 0, from_left)
        chosen, tag = select_tag(b)
        pick(b, chosen, tag, 0)
        for q in range(1, shards):
            arrive(b, q, from_left)
            pick(b, chosen, tag, q)

    def project(b, k, last):
        tile = tile_of(cols)

        def step(j, carry):
            at = pl.ds(pl.multiple_of(j * tile, tile), tile)
            term = jnp.dot(
                x[b, :, pl.ds(META + k * half, half)], w[pl.ds(k * half, half), at],
                preferred_element_type=F32,
            )
            if last:
                base[b, :, at] = (acc[b, :, at] + term).astype(BF16)
            else:
                acc[b, :, at] = term
            return carry

        lax.fori_loop(0, cols // tile, step, 0)

    mine_cols = pl.ds(pl.multiple_of(p * cols, 128), cols)
    mine_slots = pl.ds(pl.multiple_of(p * SLOTS, SLOTS), SLOTS)

    def base_copy(b):
        return rcopy(base.at[b], home_base.at[:, mine_cols], bsend.at[b], brecv.at[p], b, me)

    def delta_copy(b, sh):
        return rcopy(
            delta.at[b, sh], home_delta.at[me, mine_slots], dsend.at[b, sh], drecv.at[p, me], b, sh
        )

    lane = lax.broadcasted_iota(jnp.int32, (many, 256), 1) // ranks
    lower = lax.broadcasted_iota(jnp.int32, (many // 2, 128), 1) < 64

    def adapter_of(b):
        tag = rows[b, :, :, pl.ds(0, META)].reshape(many, META).astype(F32)
        return tag[:, 1:2].astype(jnp.int32)

    def shrink(b):
        for sh in peers:
            rcopy(rows.at[b, sh], rows.at[b, sh], rsend.at[b, sh], rrecv.at[b, sh], p, sh).wait_recv()
        adapter = adapter_of(b)
        here = rows[b, :, :, pl.ds(META, part)].reshape(many, part)
        total = jnp.zeros((many, 128), F32)
        for j in range(tiles):
            term = lax.dot_general(
                here, dn[pl.ds(j * 256, 256), :], (((1,), (1,)), ((), ())),
                preferred_element_type=F32,
            )
            term = jnp.where(lane + j * each == adapter, term, 0.0)
            total = total + term[:, :128] + term[:, 128:]
        total = total + pltpu.roll(total, 64, 1)
        packed = jnp.where(lower, total[: many // 2], total[many // 2 :])
        low_out[b] = packed
        low[b, me] = packed
        for sh in peers:
            rcopy(low_out.at[b], low.at[b, me], lsend.at[b, sh], lrecv.at[b, me], p, sh).start()

    def grow(b):
        for sh in peers:
            rcopy(low_out.at[b], low.at[b, sh], lsend.at[b, sh], lrecv.at[b, sh], p, sh).wait_recv()
        adapter = adapter_of(b)
        both = low[b, 0]
        for sh in range(1, shards):
            both = both + low[b, sh]
        both = both.astype(BF16).astype(F32)
        turned = pltpu.roll(both, 64, 1)
        full = jnp.concatenate(
            [jnp.where(lower, both, turned), jnp.where(lower, turned, both)], axis=0
        )
        full = jnp.concatenate([full, full], axis=1)
        spread = jnp.concatenate(
            [
                jnp.where(lane + j * each == adapter, full, 0.0).astype(BF16)
                for j in range(tiles)
            ],
            axis=1,
        )
        rest = jnp.dot(spread, up[:, pl.ds(3 * quarter, quarter)], preferred_element_type=F32)
        top = lax.broadcasted_iota(jnp.int32, (many, quarter), 0) % SLOTS < HELD
        for j in range(3):
            at = pl.ds(j * quarter, quarter)
            term = jnp.dot(spread, up[:, at], preferred_element_type=F32)
            term = jnp.where(top, term, pltpu.roll(rest, HELD - 4 * j, 0))
            delta[b, :, :, at] = (ADAPTER_SCALE * term).astype(BF16).reshape(shards, SLOTS, quarter)
        for sh in range(shards):
            @pl.when(jnp.logical_or(b != p, sh != me))
            def _():
                delta_copy(b, sh).start()

            @pl.when(jnp.logical_and(b == p, sh == me))
            def _():
                home_delta[me, mine_slots] = delta[b, sh]

    def both_sides(t, f):
        def turn(i, c):
            b = jnp.where(i == 0, p - t, p + t)
            valid = jnp.logical_and(jnp.logical_and(b >= 0, b < pools), jnp.logical_or(i == 0, t > 0))

            @pl.when(valid)
            def _():
                f(b)
            return c

        lax.fori_loop(0, 2, turn, 0)

    chosen, tag = select_tag(p)
    for q in range(shards):
        pick(p, chosen, tag, q)

    def step(t, carry):
        @pl.when(t == 0)
        def _():
            loads[0].wait()
        both_sides(t, lambda b: project(b, 0, False))

        @pl.when(t == 0)
        def _():
            loads[2].wait()
        both_sides(t, shrink)

        @pl.when(t == 0)
        def _():
            loads[1].wait()

        def finish(b):
            project(b, 1, True)

            @pl.when(b != p)
            def _():
                base_copy(b).start()

            @pl.when(b == p)
            def _():
                home_base[:, mine_cols] = base[b]

        both_sides(t, finish)

        @pl.when(p - 1 - t >= 0)
        def _():
            receive(p - 1 - t, True)

        @pl.when(p + 1 + t < pools)
        def _():
            receive(p + 1 + t, False)

        @pl.when(t == 0)
        def _():
            loads[3].wait()
        both_sides(t, grow)
        return carry

    lax.fori_loop(0, pools, step, 0)

    slots = pools * SLOTS
    lanes = lax.broadcasted_iota(jnp.int32, (rows_dev, slots), 1)
    owner = jnp.where(owner_column == lanes // SLOTS, 1.0, 0.0)
    after = jnp.where(down_axis > along, 1.0, 0.0).astype(BF16)
    rank = jnp.dot(after, owner.astype(BF16), preferred_element_type=F32)
    seat = lanes % SLOTS
    place = jnp.where(rank == seat.astype(F32), owner, 0.0).astype(BF16)
    tails = [
        jnp.where(
            jnp.logical_and(seat >= HELD, rank == (seat - HELD + 4 * k).astype(F32)), owner, 0.0
        ).astype(BF16)
        for k in range(3)
    ]

    def base_wait(z, carry):
        @pl.when(z != p)
        def _():
            dst = home_base.at[:, pl.ds(pl.multiple_of(z * cols, 128), cols)]
            rcopy(base.at[z], dst, bsend.at[z], brecv.at[z], z, me).wait_recv()
        return carry

    lax.fori_loop(0, pools, base_wait, 0)

    for sh in range(shards):
        def delta_wait(z, carry):
            @pl.when(jnp.logical_or(z != p, sh != me))
            def _():
                dst = home_delta.at[sh, pl.ds(pl.multiple_of(z * SLOTS, SLOTS), SLOTS)]
                rcopy(delta.at[z, sh], dst, dsend.at[z, sh], drecv.at[z, sh], z, sh).wait_recv()
            return carry

        lax.fori_loop(0, pools, delta_wait, 0)
        start = sh * part
        wide = 3 * quarter
        term = jnp.dot(place, home_delta[sh], preferred_element_type=F32)
        at = pl.ds(start, wide)
        out_ref[:, at] = (home_base[:, at].astype(F32) + term).astype(BF16)
        term = jnp.zeros((rows_dev, quarter), F32)
        for k in range(3):
            term = term + jnp.dot(
                tails[k], home_delta[sh, :, pl.ds(k * quarter, quarter)], preferred_element_type=F32
            )
        at = pl.ds(start + wide, quarter)
        out_ref[:, at] = (home_base[:, at].astype(F32) + term).astype(BF16)

    def drain(b, carry):
        for q in range(shards):
            @pl.when(jnp.logical_and(b <= p, p + 1 < pools))
            def _():
                to_right(b, q).wait_send()

            @pl.when(jnp.logical_and(b >= p, p >= 1))
            def _():
                to_left(b, q).wait_send()

            @pl.when(q != me)
            def _():
                rcopy(picked.at[b, q], rows.at[b, me], rsend.at[b, q], rrecv.at[b, me], p, q).wait_send()
                rcopy(low_out.at[b], low.at[b, me], lsend.at[b, q], lrecv.at[b, me], p, q).wait_send()

            @pl.when(jnp.logical_or(b != p, q != me))
            def _():
                delta_copy(b, q).wait_send()

        @pl.when(b != p)
        def _():
            base_copy(b).wait_send()
        return carry

    lax.fori_loop(0, pools, drain, 0)


def local(hidden, query_weight_matrix, adapter_down_weight, adapter_up_weight, adapter_index_rows):
    pools = lax.axis_size("pool")
    chips = lax.axis_size("chip")
    shards = lax.axis_size("sub") * chips
    row_count, width = hidden.shape
    cols = query_weight_matrix.shape[1]
    stack, ranks, part = adapter_down_weight.shape
    if 2 + row_count // (pools - 1) > HELD:
        raise ValueError("owner overflow")
    dma = pltpu.SemaphoreType.DMA
    vmem = pl.BlockSpec(memory_space=pltpu.VMEM)
    hbm = pl.BlockSpec(memory_space=pl.ANY)
    return pl.pallas_call(
        functools.partial(kernel, pools, chips, shards, stack),
        out_shape=jax.ShapeDtypeStruct((row_count, width), BF16),
        in_specs=[hbm, vmem, hbm, hbm, hbm],
        out_specs=vmem,
        scratch_shapes=[
            pltpu.VMEM((pools, row_count, META + width), BF16),
            pltpu.VMEM((width, cols), BF16),
            pltpu.VMEM((stack * ranks, part), BF16),
            pltpu.VMEM((stack * ranks, part), BF16),
            pltpu.VMEM((pools, shards, SLOTS, META + part), BF16),
            pltpu.VMEM((pools, shards, SLOTS, META + part), BF16),
            pltpu.VMEM((pools, shards * SLOTS // 2, 128), F32),
            pltpu.VMEM((pools, shards, shards * SLOTS // 2, 128), F32),
            pltpu.VMEM((pools, shards, SLOTS, part - part // 4), BF16),
            pltpu.VMEM((shards, pools * SLOTS, part - part // 4), BF16),
            pltpu.VMEM((pools, row_count, cols), BF16),
            pltpu.VMEM((row_count, width), BF16),
            pltpu.VMEM((pools, row_count, cols), F32),
            dma((5,)),
            dma((pools, shards)),
            dma((pools, shards)),
            dma((pools, shards)),
            dma((pools, shards)),
            dma((pools, shards)),
            dma((pools, shards)),
            dma((pools, shards)),
            dma((pools,)),
            dma((pools,)),
            dma((pools, shards)),
            dma((pools, shards)),
        ],
        compiler_params=pltpu.CompilerParams(
            collective_id=0, has_side_effects=True, vmem_limit_bytes=56 * 1024 * 1024
        ),
    )(
        hidden,
        adapter_index_rows[None, :],
        query_weight_matrix,
        adapter_down_weight.reshape(stack * ranks, part),
        adapter_up_weight.reshape(stack * ranks, part),
    )


def solution(mesh):
    in_specs = (
        P(("groups", "pool", "sub", "chip"), None),
        P(None, "pool"),
        P("pool", None, ("sub", "chip")),
        P("pool", None, ("sub", "chip")),
        P(("groups", "pool", "sub", "chip")),
    )
    out_specs = P(("groups", "pool", "sub", "chip"), None)
    return jax.shard_map(local, mesh=mesh, in_specs=in_specs, out_specs=out_specs, check_vma=False)
```

time: 55.5 us -> 47.2 us (0.85); the launches traced: 54.8 us -> 47.1 us
  Pallas kernels: 50.6 us -> 45.4 us
  local copies, waits for them, and re-layouts: 4.24 us -> 1.67 us
    pallas_call x1, Pallas kernels: 50.6 us -> 45.4 us  [local(): pl.pallas_call(functools.partial(kernel, pools, chips, shards, stack), ou...]
    broadcast_in_dim x1 -> x0, local copies, waits for them, and re-layouts: 1.34 us -> none  [local(): adapter_index_rows[:, None]]
    pad x1 -> x0, local copies, waits for them, and re-layouts: 1.23 us -> none  [local(): jnp.pad(adapter_index_rows[None, :], ((0, 0), (0, 128 - row_count)))]
where the time goes in v2:
time: 47.2 us; the launch traced here: 47.1 us
  Pallas kernels  45.4 us (96%)
  local copies, waits for them, and re-layouts  1.67 us (4%)
    pallas_call x1, Pallas kernels, local(): pl.pallas_call(functools.partial(kernel, pools, chips, shards, stack), ou...  45.4 us
    unnamed x1, local copies, waits for them, and re-layouts  1.67 us

profile of v2, /device:TPU:0, one launch (start us, length us, event | category | flops | bytes accessed | tf_op | source)
XLA Modules:
  0.0 47.1 jit_solution(7731258888121182133)
XLA Ops:
  0.0 45.4 %shard_map.55 = bf16[32,4096]{1,0:T(8,128)(2,1)} custom-call(bf16[32,4096]{1,0:T(8,128)(2,1)} %h_hbm.1, s32[1,32]{1,0:T(1,128)} %bitcast.5, bf16[4096,1024]{1,0:T(8,128)(2,1)} %w_hbm.1, bf16[1024,1024]{1,0:T(8,128)(2,1)} %bitcast.3, bf16[1024,1024]{1,0:T(8,128)(2,1)} %bitcast.4), custom_call_target="tpu_custom_call" | custom-call | tf_op jit(solution)/shard_map/pallas_call | solution.py:404
  45.4 1.7 %copy.7 = bf16[32,4096]{1,0:T(8,128)(2,1)} copy(bf16[32,4096]{1,0:T(8,128)(2,1)} %shard_map.55) | data formatting | bytes 524288

commit v3 on v2

--- a/solution.py
+++ b/solution.py
@@ -23,7 +23,7 @@
 def kernel(
     pools, chips, shards, stack,
     h_hbm, idx_ref, w_hbm, dn_hbm, up_hbm, out_ref,
-    x, w, dn, up, picked, rows, low_out, low, delta, home_delta, base, home_base, acc,
+    x, w, dn, up, chosen, tags, picked, rows, low_out, low, delta, home_delta, base, home_base, acc,
     wsem, hright, hleft, hrecv, rsend, rrecv, lsend, lrecv, bsend, brecv, dsend, drecv,
 ):
     p = lax.axis_index("pool")
@@ -126,62 +126,51 @@
         slot = lax.broadcasted_iota(jnp.int32, (SLOTS, rows_dev), 0).astype(F32)
         return jnp.where(rank == slot, owned, 0.0).astype(BF16)
 
-    def pick(b, chosen, tag, q):
-        got = jnp.dot(chosen, x[b, :, piece(q)], preferred_element_type=F32).astype(BF16)
+    def choose(b):
+        hit = selection(b)
+        chosen[b] = hit
+        tags[b] = jnp.dot(hit, x[b, :, pl.ds(0, META)], preferred_element_type=F32).astype(BF16)
+
+    def pick(b, q):
+        got = jnp.dot(chosen[b], x[b, :, piece(q)], preferred_element_type=F32).astype(BF16)
 
         @pl.when(q != me)
         def _():
-            picked[b, q, :, pl.ds(0, META)] = tag
+            picked[b, q, :, pl.ds(0, META)] = tags[b]
             picked[b, q, :, pl.ds(META, part)] = got
             rcopy(picked.at[b, q], rows.at[b, me], rsend.at[b, q], rrecv.at[b, me], p, q).start()
 
         @pl.when(q == me)
         def _():
-            rows[b, me, :, pl.ds(0, META)] = tag
+            rows[b, me, :, pl.ds(0, META)] = tags[b]
             rows[b, me, :, pl.ds(META, part)] = got
 
-    def select_tag(b):
-        chosen = selection(b)
-        tag = jnp.dot(chosen, x[b, :, pl.ds(0, META)], preferred_element_type=F32).astype(BF16)
-        return chosen, tag
-
-    def arrive(b, q, from_left):
+    def arrive(b, q):
         rcopy(
             x.at[b, :, sent(q)], x.at[b, :, sent(q)], hright.at[b, q], hrecv.at[b, q], p, peers[0]
         ).wait_recv()
-        if from_left:
-            @pl.when(p + 1 < pools)
-            def _():
-                to_right(b, q).start()
-        else:
-            @pl.when(p >= 1)
-            def _():
-                to_left(b, q).start()
-
-    def receive(b, from_left):
-        arrive(b, 0, from_left)
-        chosen, tag = select_tag(b)
-        pick(b, chosen, tag, 0)
-        for q in range(1, shards):
-            arrive(b, q, from_left)
-            pick(b, chosen, tag, q)
-
-    def project(b, k, last):
+
+        @pl.when(jnp.logical_and(b < p, p + 1 < pools))
+        def _():
+            to_right(b, q).start()
+
+        @pl.when(jnp.logical_and(b > p, p >= 1))
+        def _():
+            to_left(b, q).start()
+
+    def project(b, q):
         tile = tile_of(cols)
-
-        def step(j, carry):
-            at = pl.ds(pl.multiple_of(j * tile, tile), tile)
+        for j in range(cols // tile):
+            at = pl.ds(j * tile, tile)
             term = jnp.dot(
-                x[b, :, pl.ds(META + k * half, half)], w[pl.ds(k * half, half), at],
-                preferred_element_type=F32,
+                x[b, :, piece(q)], w[pl.ds(q * part, part), at], preferred_element_type=F32
             )
-            if last:
-                base[b, :, at] = (acc[b, :, at] + term).astype(BF16)
+            if q > 0:
+                term = term + acc[b, :, at]
+            if q == shards - 1:
+                base[b, :, at] = term.astype(BF16)
             else:
                 acc[b, :, at] = term
-            return carry
-
-        lax.fori_loop(0, cols // tile, step, 0)
 
     mine_cols = pl.ds(pl.multiple_of(p * cols, 128), cols)
     mine_slots = pl.ds(pl.multiple_of(p * SLOTS, SLOTS), SLOTS)
@@ -260,7 +249,8 @@
     def both_sides(t, f):
         def turn(i, c):
             b = jnp.where(i == 0, p - t, p + t)
-            valid = jnp.logical_and(jnp.logical_and(b >= 0, b < pools), jnp.logical_or(i == 0, t > 0))
+            inside = jnp.logical_and(b >= 0, b < pools)
+            valid = jnp.logical_and(inside, jnp.logical_or(i == 0, t != 0))
 
             @pl.when(valid)
             def _():
@@ -269,27 +259,43 @@
 
         lax.fori_loop(0, 2, turn, 0)
 
-    chosen, tag = select_tag(p)
-    for q in range(shards):
-        pick(p, chosen, tag, q)
-
     def step(t, carry):
-        @pl.when(t == 0)
-        def _():
-            loads[0].wait()
-        both_sides(t, lambda b: project(b, 0, False))
+        for q in range(shards):
+            def take(b):
+                @pl.when(b != p)
+                def _():
+                    arrive(b, q)
+                if q == 0:
+                    choose(b)
+                pick(b, q)
+
+            both_sides(t, take)
+            if q == 1:
+                @pl.when(t == 0)
+                def _():
+                    loads[0].wait()
+            if q == 3:
+                @pl.when(t == 0)
+                def _():
+                    loads[1].wait()
+            if q > 0:
+                both_sides(t, lambda b: project(b, q - 1))
+            if q == 0:
+                @pl.when(t == 1)
+                def _():
+                    loads[3].wait()
+
+                @pl.when(t > 0)
+                def _():
+                    both_sides(t - 1, grow)
 
         @pl.when(t == 0)
         def _():
             loads[2].wait()
         both_sides(t, shrink)
 
-        @pl.when(t == 0)
-        def _():
-            loads[1].wait()
-
         def finish(b):
-            project(b, 1, True)
+            project(b, shards - 1)
 
             @pl.when(b != p)
             def _():
@@ -300,22 +306,10 @@
                 home_base[:, mine_cols] = base[b]
 
         both_sides(t, finish)
-
-        @pl.when(p - 1 - t >= 0)
-        def _():
-            receive(p - 1 - t, True)
-
-        @pl.when(p + 1 + t < pools)
-        def _():
-            receive(p + 1 + t, False)
-
-        @pl.when(t == 0)
-        def _():
-            loads[3].wait()
-        both_sides(t, grow)
         return carry
 
     lax.fori_loop(0, pools, step, 0)
+    both_sides(pools - 1, grow)
 
     slots = pools * SLOTS
     lanes = lax.broadcasted_iota(jnp.int32, (rows_dev, slots), 1)
@@ -331,6 +325,8 @@
         for k in range(3)
     ]
 
+    places = jnp.concatenate([place] + tails, axis=0)
+
     def base_wait(z, carry):
         @pl.when(z != p)
         def _():
@@ -351,16 +347,14 @@
         lax.fori_loop(0, pools, delta_wait, 0)
         start = sh * part
         wide = 3 * quarter
-        term = jnp.dot(place, home_delta[sh], preferred_element_type=F32)
+        term = jnp.dot(places, home_delta[sh], preferred_element_type=F32)
         at = pl.ds(start, wide)
-        out_ref[:, at] = (home_base[:, at].astype(F32) + term).astype(BF16)
-        term = jnp.zeros((rows_dev, quarter), F32)
-        for k in range(3):
-            term = term + jnp.dot(
-                tails[k], home_delta[sh, :, pl.ds(k * quarter, quarter)], preferred_element_type=F32
-            )
+        out_ref[:, at] = (home_base[:, at].astype(F32) + term[:rows_dev]).astype(BF16)
+        rest = term[rows_dev : 2 * rows_dev, :quarter]
+        rest = rest + term[2 * rows_dev : 3 * rows_dev, quarter : 2 * quarter]
+        rest = rest + term[3 * rows_dev :, 2 * quarter :]
         at = pl.ds(start + wide, quarter)
-        out_ref[:, at] = (home_base[:, at].astype(F32) + term).astype(BF16)
+        out_ref[:, at] = (home_base[:, at].astype(F32) + rest).astype(BF16)
 
     def drain(b, carry):
         for q in range(shards):
@@ -411,6 +405,8 @@
             pltpu.VMEM((width, cols), BF16),
             pltpu.VMEM((stack * ranks, part), BF16),
             pltpu.VMEM((stack * ranks, part), BF16),
+            pltpu.VMEM((pools, SLOTS, row_count), BF16),
+            pltpu.VMEM((pools, SLOTS, META), BF16),
             pltpu.VMEM((pools, shards, SLOTS, META + part), BF16),
             pltpu.VMEM((pools, shards, SLOTS, META + part), BF16),
             pltpu.VMEM((pools, shards * SLOTS // 2, 128), F32),

time: 47.2 us -> 49.3 us (1.044)
  Pallas kernels: 45.4 us -> 47.5 us
    pallas_call x1, Pallas kernels: 45.4 us -> 47.5 us  [local(): pl.pallas_call(functools.partial(kernel, pools, chips, shards, stack), ou...]
where the time goes in v3:
time: 49.3 us; the launch traced here: 49.2 us
  Pallas kernels  47.5 us (96%)
  local copies, waits for them, and re-layouts  1.67 us (3%)
    pallas_call x1, Pallas kernels, local(): pl.pallas_call(functools.partial(kernel, pools, chips, shards, stack), ou...  47.5 us
    unnamed x1, local copies, waits for them, and re-layouts  1.67 us

profile of v3, /device:TPU:0, one launch (start us, length us, event | category | flops | bytes accessed | tf_op | source)
XLA Modules:
  0.0 49.2 jit_solution(2406177272044424730)
XLA Ops:
  0.0 47.5 %shard_map.55 = bf16[32,4096]{1,0:T(8,128)(2,1)} custom-call(bf16[32,4096]{1,0:T(8,128)(2,1)} %h_hbm.1, s32[1,32]{1,0:T(1,128)} %bitcast.5, bf16[4096,1024]{1,0:T(8,128)(2,1)} %w_hbm.1, bf16[1024,1024]{1,0:T(8,128)(2,1)} %bitcast.3, bf16[1024,1024]{1,0:T(8,128)(2,1)} %bitcast.4), custom_call_target="tpu_custom_call" | custom-call | tf_op jit(solution)/shard_map/pallas_call | solution.py:398
  47.5 1.7 %copy.7 = bf16[32,4096]{1,0:T(8,128)(2,1)} copy(bf16[32,4096]{1,0:T(8,128)(2,1)} %shard_map.55) | data formatting | bytes 524288

commit v4 on v2

--- a/solution.py
+++ b/solution.py
@@ -169,8 +169,8 @@
     def project(b, k, last):
         tile = tile_of(cols)
 
-        def step(j, carry):
-            at = pl.ds(pl.multiple_of(j * tile, tile), tile)
+        for j in range(cols // tile):
+            at = pl.ds(j * tile, tile)
             term = jnp.dot(
                 x[b, :, pl.ds(META + k * half, half)], w[pl.ds(k * half, half), at],
                 preferred_element_type=F32,
@@ -179,9 +179,6 @@
                 base[b, :, at] = (acc[b, :, at] + term).astype(BF16)
             else:
                 acc[b, :, at] = term
-            return carry
-
-        lax.fori_loop(0, cols // tile, step, 0)
 
     mine_cols = pl.ds(pl.multiple_of(p * cols, 128), cols)
     mine_slots = pl.ds(pl.multiple_of(p * SLOTS, SLOTS), SLOTS)
@@ -299,15 +296,25 @@
             def _():
                 home_base[:, mine_cols] = base[b]
 
-        both_sides(t, finish)
-
-        @pl.when(p - 1 - t >= 0)
-        def _():
-            receive(p - 1 - t, True)
-
-        @pl.when(p + 1 + t < pools)
-        def _():
-            receive(p + 1 + t, False)
+        inner = jnp.logical_and(jnp.logical_and(p - t >= 0, p + t < pools), t > 0)
+
+        def phase(i, c):
+            @pl.when(i == jnp.where(inner, 1, 0))
+            def _():
+                both_sides(t, finish)
+
+            @pl.when(i == jnp.where(inner, 0, 1))
+            def _():
+                @pl.when(p - 1 - t >= 0)
+                def _():
+                    receive(p - 1 - t, True)
+
+                @pl.when(p + 1 + t < pools)
+                def _():
+                    receive(p + 1 + t, False)
+            return c
+
+        lax.fori_loop(0, 2, phase, 0)
 
         @pl.when(t == 0)
         def _():
@@ -331,6 +338,8 @@
         for k in range(3)
     ]
 
+    places = jnp.concatenate([place] + tails, axis=0)
+
     def base_wait(z, carry):
         @pl.when(z != p)
         def _():
@@ -351,16 +360,14 @@
         lax.fori_loop(0, pools, delta_wait, 0)
         start = sh * part
         wide = 3 * quarter
-        term = jnp.dot(place, home_delta[sh], preferred_element_type=F32)
+        term = jnp.dot(places, home_delta[sh], preferred_element_type=F32)
         at = pl.ds(start, wide)
-        out_ref[:, at] = (home_base[:, at].astype(F32) + term).astype(BF16)
-        term = jnp.zeros((rows_dev, quarter), F32)
-        for k in range(3):
-            term = term + jnp.dot(
-                tails[k], home_delta[sh, :, pl.ds(k * quarter, quarter)], preferred_element_type=F32
-            )
+        out_ref[:, at] = (home_base[:, at].astype(F32) + term[:rows_dev]).astype(BF16)
+        rest = term[rows_dev : 2 * rows_dev, :quarter]
+        rest = rest + term[2 * rows_dev : 3 * rows_dev, quarter : 2 * quarter]
+        rest = rest + term[3 * rows_dev :, 2 * quarter :]
         at = pl.ds(start + wide, quarter)
-        out_ref[:, at] = (home_base[:, at].astype(F32) + term).astype(BF16)
+        out_ref[:, at] = (home_base[:, at].astype(F32) + rest).astype(BF16)
 
     def drain(b, carry):
         for q in range(shards):

time: 47.2 us -> 41.5 us (0.88)
  Pallas kernels: 45.4 us -> 39.6 us
    pallas_call x1, Pallas kernels: 45.4 us -> 39.6 us  [local(): pl.pallas_call(functools.partial(kernel, pools, chips, shards, stack), ou...]
where the time goes in v4:
time: 41.5 us; the launch traced here: 41.3 us
  Pallas kernels  39.6 us (95%)
  local copies, waits for them, and re-layouts  1.67 us (4%)
    pallas_call x1, Pallas kernels, local(): pl.pallas_call(functools.partial(kernel, pools, chips, shards, stack), ou...  39.6 us
    unnamed x1, local copies, waits for them, and re-layouts  1.67 us

profile of v4, /device:TPU:0, one launch (start us, length us, event | category | flops | bytes accessed | tf_op | source)
XLA Modules:
  0.0 41.3 jit_solution(4237453459949205263)
XLA Ops:
  0.0 39.6 %shard_map.55 = bf16[32,4096]{1,0:T(8,128)(2,1)} custom-call(bf16[32,4096]{1,0:T(8,128)(2,1)} %h_hbm.1, s32[1,32]{1,0:T(1,128)} %bitcast.5, bf16[4096,1024]{1,0:T(8,128)(2,1)} %w_hbm.1, bf16[1024,1024]{1,0:T(8,128)(2,1)} %bitcast.3, bf16[1024,1024]{1,0:T(8,128)(2,1)} %bitcast.4), custom_call_target="tpu_custom_call" | custom-call | tf_op jit(solution)/shard_map/pallas_call | solution.py:411
  39.6 1.7 %copy.7 = bf16[32,4096]{1,0:T(8,128)(2,1)} copy(bf16[32,4096]{1,0:T(8,128)(2,1)} %shard_map.55) | data formatting | bytes 524288
